TPU v7x, 128 devices: a whole 4x4x4 slice. The times are simulated.
128 devices in a mesh: row: 16 (over x_hi, y, core), col: 8 (over x_lo, z).
Axes of the slice: x: 4 (x_hi: 2, x_lo: 2; x = x_hi * 2 + x_lo), y: 4, z: 4, core: 2. Of those that a mesh axis runs over, the one named last changes fastest.
Arguments:
- points: bfloat16 [65536, 128], P(('row', 'col')), may hold values from -6 to 6
- probes: bfloat16 [65536, 128], P(('row', 'col')), may hold values from -6 to 6
Outputs:
- sketch: float32 [65536, 128], P(('row', 'col'))
- basis: float32 [65536, 128], P(('row', 'col'))
All inputs are finite; a program needn't handle non-finite values.
Results may differ from a plain program's by a relative error of at most 0.0044.
Values may be sent and summed in bfloat16 or wider, within the bound.
No kernel may reach another device: no remote copies, remote signals or barrier semaphores. Data moves between devices by JAX's collectives and lax.ppermute only.
A program may use at most 64 MiB of HBM per device.

v0:
```python
import math
import jax
import jax.numpy as jnp
from jax import lax
from jax.sharding import PartitionSpec as P


def shards(points, probes):
    own_count = points.shape[0]
    width = points.shape[1]
    nprobe = probes.shape[1]
    factor = -3.0 / width
    row_pts = lax.all_gather(points, "col", axis=0, tiled=True)
    row_sq = jnp.sum(jnp.square(row_pts.astype(jnp.float32)), axis=1)
    nrows = row_pts.shape[0]
    block = math.gcd(nrows, 512)
    nblocks = nrows // block
    blocked = row_pts.reshape(nblocks, block, width)
    sq_blocked = row_sq.reshape(nblocks, block)
    start_sum = jnp.zeros((nrows, nprobe), jnp.float32)
    col_pts = lax.all_gather(points, "row", axis=0, tiled=True)
    col_probe = lax.all_gather(probes, "row", axis=0, tiled=True)
    col_sq = jnp.sum(jnp.square(col_pts.astype(jnp.float32)), axis=1)

    def one_block(args):
        rows, sq_rows = args
        cross = lax.dot_general(
            rows, col_pts, (((1,), (1,)), ((), ())), preferred_element_type=jnp.float32
        )
        expo = (sq_rows[:, None] + col_sq[None, :] - 2.0 * cross) * factor
        kernel = jnp.exp(expo).astype(jnp.bfloat16)
        return jnp.dot(kernel, col_probe, preferred_element_type=jnp.float32)

    terms = lax.map(one_block, (blocked, sq_blocked))
    partial_rows = terms.reshape(nrows, start_sum.shape[1])
    total = lax.psum(partial_rows, "col")
    own_rows = lax.dynamic_slice_in_dim(total, lax.axis_index("col") * own_count, own_count, 0)
    all_points = own_count * lax.axis_size("row") * lax.axis_size("col")
    gram_part = jnp.dot(
        own_rows.T, own_rows, precision=lax.Precision.HIGHEST, preferred_element_type=jnp.float32
    )
    gram = lax.psum(gram_part, ("row", "col"))
    lower = jnp.linalg.cholesky(gram)
    solved = jax.scipy.linalg.solve_triangular(lower, own_rows.T, lower=True)
    basis = solved.T * math.sqrt(all_points)
    return (own_rows, basis)


def solution(mesh):
    in_specs = (P(("row", "col"), None), P(("row", "col"), None))
    out_specs = (P(("row", "col"), None), P(("row", "col"), None))
    return jax.shard_map(shards, mesh=mesh, in_specs=in_specs, out_specs=out_specs, check_vma=False)
```

profile of v0, /device:TPU:1, one launch (start us, length us, event | category | flops | bytes accessed | tf_op | source)
XLA Modules:
  0.0 462.9 jit_solution(4579630985239570801)
XLA Ops:
  7.9 0.7 all-gather.6.cloned.1.call-update
  9.4 37.8 %all-gather.4.cloned.1.call-done = bf16[4096,128]{1,0:T(8,128)(2,1)} async-done(((bf16[512,128]{1,0:T(8,128)(2,1)}), bf16[4096,128]{1,0:T(8,128)(2,1)}) %all-gather.4.cloned.1.call-update) | async-done | bytes 1048592 | tf_op jit(solution)/shard_map/all_gather | solution.py:13
  47.2 1.8 multiply_reduce_fusion.1
  49.1 52.3 %all-gather.6.cloned.1.call-done = bf16[8192,128]{1,0:T(8,128)(2,1)} async-done(((bf16[512,128]{1,0:T(8,128)(2,1)}), bf16[8192,128]{1,0:T(8,128)(2,1)}) %all-gather.6.cloned.1.call-update) | async-done | bytes 2097168 | tf_op jit(solution)/shard_map/all_gather | solution.py:21
  101.4 2.9 multiply_reduce_fusion
  104.3 45.9 %all-gather.8.cloned.1.call-done = bf16[8192,128]{1,0:T(8,128)(2,1)} async-done(((bf16[512,128]{1,0:T(8,128)(2,1)}), bf16[8192,128]{1,0:T(8,128)(2,1)}) %all-gather.8.cloned.1.call-update) | async-done | bytes 2097168 | tf_op jit(solution)/shard_map/all_gather | solution.py:22
  150.2 56.3 %while.10 = (s32[]{:T(128)}, f32[8,512,128]{2,1,0:T(8,128)}, f32[8,512]{1,0:T(8,128)S(1)}, f32[8192]{0:T(1024)S(1)}, bf16[8,512,128]{2,1,0:T(8,128)(2,1)}, /*ind...) while((s32[]{:T(128)}, f32[8,512,128]{2,1,0:T(8,128)}, f32[8,512]{1,0:T(8,128)S(1)}, ...), condition=%wide.region_3.4_spmd, body=%wide.region_2.3_spmd.sunk | while | flops 2168455168 | bytes 4627545 | solution.py:34
  150.2 7.0 %fusion.27 = f32[8,512,128]{2,1,0:T(8,128)} fusion(f32[8,512,128]{2,1,0:T(8,128)} %get-tuple-element.106, s32[]{:T(128)} %get-tuple-element.105, bf16[8192,128]{1,0:T(8,128)(2,1)} %get-tuple-element.119, bf16[8192,128]{1,0:T(8,128)(2,1)S(1)} %get-tuple-element.118, f32[8192]{0:T(1024)S(1)} %get-tuple-element.116, f32[512]{0:T(512)S(1)} %bitcast.37, ...), kind=kOutput, calls=%fused_computation.3.clone.1 | convolution fusion | flops 2168455168 | bytes 4623360 | tf_op jit(solution)/shard_map/while/body/eval_jaxpr/dot_general | solution.py:32
  157.2 7.0 %fusion.27 = f32[8,512,128]{2,1,0:T(8,128)} fusion(f32[8,512,128]{2,1,0:T(8,128)} %get-tuple-element.106, s32[]{:T(128)} %get-tuple-element.105, bf16[8192,128]{1,0:T(8,128)(2,1)} %get-tuple-element.119, bf16[8192,128]{1,0:T(8,128)(2,1)S(1)} %get-tuple-element.118, f32[8192]{0:T(1024)S(1)} %get-tuple-element.116, f32[512]{0:T(512)S(1)} %bitcast.37, ...), kind=kOutput, calls=%fused_computation.3.clone.1 | convolution fusion | flops 2168455168 | bytes 4623360 | tf_op jit(solution)/shard_map/while/body/eval_jaxpr/dot_general | solution.py:32
  164.3 7.0 %fusion.27 = f32[8,512,128]{2,1,0:T(8,128)} fusion(f32[8,512,128]{2,1,0:T(8,128)} %get-tuple-element.106, s32[]{:T(128)} %get-tuple-element.105, bf16[8192,128]{1,0:T(8,128)(2,1)} %get-tuple-element.119, bf16[8192,128]{1,0:T(8,128)(2,1)S(1)} %get-tuple-element.118, f32[8192]{0:T(1024)S(1)} %get-tuple-element.116, f32[512]{0:T(512)S(1)} %bitcast.37, ...), kind=kOutput, calls=%fused_computation.3.clone.1 | convolution fusion | flops 2168455168 | bytes 4623360 | tf_op jit(solution)/shard_map/while/body/eval_jaxpr/dot_general | solution.py:32
  171.3 7.0 %fusion.27 = f32[8,512,128]{2,1,0:T(8,128)} fusion(f32[8,512,128]{2,1,0:T(8,128)} %get-tuple-element.106, s32[]{:T(128)} %get-tuple-element.105, bf16[8192,128]{1,0:T(8,128)(2,1)} %get-tuple-element.119, bf16[8192,128]{1,0:T(8,128)(2,1)S(1)} %get-tuple-element.118, f32[8192]{0:T(1024)S(1)} %get-tuple-element.116, f32[512]{0:T(512)S(1)} %bitcast.37, ...), kind=kOutput, calls=%fused_computation.3.clone.1 | convolution fusion | flops 2168455168 | bytes 4623360 | tf_op jit(solution)/shard_map/while/body/eval_jaxpr/dot_general | solution.py:32
  178.3 7.0 %fusion.27 = f32[8,512,128]{2,1,0:T(8,128)} fusion(f32[8,512,128]{2,1,0:T(8,128)} %get-tuple-element.106, s32[]{:T(128)} %get-tuple-element.105, bf16[8192,128]{1,0:T(8,128)(2,1)} %get-tuple-element.119, bf16[8192,128]{1,0:T(8,128)(2,1)S(1)} %get-tuple-element.118, f32[8192]{0:T(1024)S(1)} %get-tuple-element.116, f32[512]{0:T(512)S(1)} %bitcast.37, ...), kind=kOutput, calls=%fused_computation.3.clone.1 | convolution fusion | flops 2168455168 | bytes 4623360 | tf_op jit(solution)/shard_map/while/body/eval_jaxpr/dot_general | solution.py:32
  185.4 7.0 %fusion.27 = f32[8,512,128]{2,1,0:T(8,128)} fusion(f32[8,512,128]{2,1,0:T(8,128)} %get-tuple-element.106, s32[]{:T(128)} %get-tuple-element.105, bf16[8192,128]{1,0:T(8,128)(2,1)} %get-tuple-element.119, bf16[8192,128]{1,0:T(8,128)(2,1)S(1)} %get-tuple-element.118, f32[8192]{0:T(1024)S(1)} %get-tuple-element.116, f32[512]{0:T(512)S(1)} %bitcast.37, ...), kind=kOutput, calls=%fused_computation.3.clone.1 | convolution fusion | flops 2168455168 | bytes 4623360 | tf_op jit(solution)/shard_map/while/body/eval_jaxpr/dot_general | solution.py:32
  192.4 7.0 %fusion.27 = f32[8,512,128]{2,1,0:T(8,128)} fusion(f32[8,512,128]{2,1,0:T(8,128)} %get-tuple-element.106, s32[]{:T(128)} %get-tuple-element.105, bf16[8192,128]{1,0:T(8,128)(2,1)} %get-tuple-element.119, bf16[8192,128]{1,0:T(8,128)(2,1)S(1)} %get-tuple-element.118, f32[8192]{0:T(1024)S(1)} %get-tuple-element.116, f32[512]{0:T(512)S(1)} %bitcast.37, ...), kind=kOutput, calls=%fused_computation.3.clone.1 | convolution fusion | flops 2168455168 | bytes 4623360 | tf_op jit(solution)/shard_map/while/body/eval_jaxpr/dot_general | solution.py:32
  199.4 7.0 %fusion.27 = f32[8,512,128]{2,1,0:T(8,128)} fusion(f32[8,512,128]{2,1,0:T(8,128)} %get-tuple-element.106, s32[]{:T(128)} %get-tuple-element.105, bf16[8192,128]{1,0:T(8,128)(2,1)} %get-tuple-element.119, bf16[8192,128]{1,0:T(8,128)(2,1)S(1)} %get-tuple-element.118, f32[8192]{0:T(1024)S(1)} %get-tuple-element.116, f32[512]{0:T(512)S(1)} %bitcast.37, ...), kind=kOutput, calls=%fused_computation.3.clone.1 | convolution fusion | flops 2168455168 | bytes 4623360 | tf_op jit(solution)/shard_map/while/body/eval_jaxpr/dot_general | solution.py:32
  206.7 77.0 %all-reduce.3.cloned.1.call-done = f32[4096,128]{1,0:T(8,128)} async-done(((f32[4096,128]{1,0:T(8,128)}), f32[4096,128]{1,0:T(8,128)}) %all-reduce.3.cloned.1.call-update) | async-done | bytes 2097168 | tf_op jit(solution)/shard_map/psum | solution.py:36
  283.8 1.0 constant_dynamic-slice_fusion.1
  284.8 1.2 fusion.14
  286.0 144.6 %all-reduce.5.cloned.1.call-done = f32[128,128]{0,1:T(8,128)} async-done(((f32[128,128]{0,1:T(8,128)}), f32[128,128]{0,1:T(8,128)}) %all-reduce.5.cloned.1.call-update) | async-done | bytes 65552 | tf_op jit(solution)/shard_map/psum | solution.py:42
  430.6 0.9 copy.5
  431.5 0.9 fusion.13
  432.4 11.7 %cholesky.16 = f32[128,128]{1,0:T(8,128)S(1)} custom-call(f32[128,128]{1,0:T(8,128)S(1)} %fusion.13), custom_call_target="Cholesky" | custom-call | tf_op jit(solution)/shard_map/jit(cholesky)/cholesky | solution.py:43
  445.4 9.8 %custom-call.7 = f32[1,128,128]{1,2,0:T(8,128)S(1)} custom-call(f32[1,128,128]{2,1,0:T(8,128)S(1)} %fusion.11), custom_call_target="InvertDiagBlocksLowerTriangular" | custom-call | tf_op jit(solution)/shard_map/jit(_solve_triangular)/triangular_solve | solution.py:44
  455.2 1.1 convolution_multiply_fusion
  (26 shorter events, 3.2 us)
Async XLA Ops:
  7.2 40.1 %all-gather.4.cloned.1.call-start = ((), (), s32[]{:S(2)}) async-start(), calls=%async_computation | async-start | bytes 1179648 | tf_op jit(solution)/shard_map/all_gather | solution.py:13
  7.9 93.5 %all-gather.6.cloned.1.call-start = ((), (), s32[]{:S(2)}) async-start(), calls=%async_computation.1 | async-start | bytes 2228224 | tf_op jit(solution)/shard_map/all_gather | solution.py:21
  8.6 141.6 %all-gather.8.cloned.1.call-start = ((), (), s32[]{:S(2)}) async-start(), calls=%async_computation.2 | async-start | bytes 2228224 | tf_op jit(solution)/shard_map/all_gather | solution.py:22
  9.4 274.4 %all-reduce.3.cloned.1.call-start = ((), (), s32[]{:S(2)}) async-start(), calls=%async_computation.3 | async-start | bytes 4194304 | tf_op jit(solution)/shard_map/psum | solution.py:36
  101.4 48.8 %copy-start.1 = (bf16[8192,128]{1,0:T(8,128)(2,1)S(1)}, bf16[8192,128]{1,0:T(8,128)(2,1)}, u32[]{:S(2)}) copy-start(bf16[8192,128]{1,0:T(8,128)(2,1)} %all-gather.6.cloned.1.call-done) | copy-start | bytes 6291460
  206.5 224.1 %all-reduce.5.cloned.1.call-start = ((), (), s32[]{:S(2)}) async-start(), calls=%async_computation.4 | async-start | bytes 131072 | tf_op jit(solution)/shard_map/psum | solution.py:42
  284.8 171.6 %copy-start = (f32[512,128]{1,0:T(8,128)}, f32[512,128]{1,0:T(8,128)S(1)}, u32[]{:S(2)}) copy-start(f32[512,128]{1,0:T(8,128)S(1)} %constant_dynamic-slice_fusion.1) | copy-start | bytes 786436
Sparse Core Ops, SparseCore 0:
  9.6 37.5 all-gather.3
  49.7 51.6 all-gather.5
  103.9 46.2 all-gather.7
  206.6 77.1 all-reduce.2
  289.0 141.5 all-reduce.4
where the time goes:
time: 463 us
  waiting for transfers between devices  360 us (78%)
  matrix products  58.5 us (13%)
  other arithmetic  28.4 us (6%)
  between operations  13.9 us (3%)
    psum x1, waiting for transfers between devices, shards(): gram = lax.psum(gram_part, ('row', 'col'))  145 us
    psum x1, waiting for transfers between devices, shards(): total = lax.psum(partial_rows, 'col')  77 us
    dot_general x8, matrix products, one_block(): return jnp.dot(kernel, col_probe, preferred_element_type=jnp.float32)  56.2 us
    all_gather x1, waiting for transfers between devices, shards(): col_pts = lax.all_gather(points, 'row', axis=0, tiled=True)  52.3 us
    all_gather x1, waiting for transfers between devices, shards(): col_probe = lax.all_gather(probes, 'row', axis=0, tiled=True)  45.9 us
    all_gather x1, waiting for transfers between devices, shards(): row_pts = lax.all_gather(points, 'col', axis=0, tiled=True)  37.8 us
    another operation x3, other arithmetic, shards(): lower = jnp.linalg.cholesky(gram)  12.4 us
    another operation x2, other arithmetic, shards(): solved = jax.scipy.linalg.solve_triangular(lower, own_rows.T, lower=True)  10.5 us
  transfers between devices with their start and end apart: 5, of which 5 were waited for; matrix products, arithmetic and copies ran while one was open for 1% of the time, Pallas kernels for 0%

commit v1 on v0

--- a/solution.py
+++ b/solution.py
@@ -39,7 +39,7 @@
     gram_part = jnp.dot(
         own_rows.T, own_rows, precision=lax.Precision.HIGHEST, preferred_element_type=jnp.float32
     )
-    gram = lax.psum(gram_part, ("row", "col"))
+    gram = lax.psum(lax.psum(gram_part, "row"), "col")
     lower = jnp.linalg.cholesky(gram)
     solved = jax.scipy.linalg.solve_triangular(lower, own_rows.T, lower=True)
     basis = solved.T * math.sqrt(all_points)

time: 463 us -> 526 us (1.14)
  waiting for transfers between devices: 360 us -> 418 us
    psum x1 -> x2, waiting for transfers between devices: 145 us -> 202 us  [shards(): gram = lax.psum(lax.psum(gram_part, 'row'), 'col')]
  transfers between devices with their start and end apart: 5 -> 6, of which waited for: 5 -> 6; matrix products, arithmetic and copies ran while one was open for 1% -> 1% of each run, Pallas kernels for 0% -> 0%
where the time goes in v1:
time: 526 us; the launch traced here: 521 us
  waiting for transfers between devices  418 us (79%)
  matrix products  58.5 us (11%)
  other arithmetic  28.4 us (5%)
  between operations  14.2 us (3%)
    psum x2, waiting for transfers between devices, shards(): gram = lax.psum(lax.psum(gram_part, 'row'), 'col')  202 us
    psum x1, waiting for transfers between devices, shards(): total = lax.psum(partial_rows, 'col')  77.2 us
    dot_general x8, matrix products, one_block(): return jnp.dot(kernel, col_probe, preferred_element_type=jnp.float32)  56.2 us
    all_gather x1, waiting for transfers between devices, shards(): col_pts = lax.all_gather(points, 'row', axis=0, tiled=True)  52.3 us
    all_gather x1, waiting for transfers between devices, shards(): col_probe = lax.all_gather(probes, 'row', axis=0, tiled=True)  45.9 us
    all_gather x1, waiting for transfers between devices, shards(): row_pts = lax.all_gather(points, 'col', axis=0, tiled=True)  37.8 us
    another operation x3, other arithmetic, shards(): lower = jnp.linalg.cholesky(gram)  12.4 us
  transfers between devices with their start and end apart: 6, of which 6 were waited for; matrix products, arithmetic and copies ran while one was open for 1% of the time, Pallas kernels for 0%

profile of v1, /device:TPU:1, one launch (start us, length us, event | category | flops | bytes accessed | tf_op | source)
XLA Modules:
  0.0 521.1 jit_solution(3104737081972666881)
XLA Ops:
  9.4 37.8 %all-gather.4.cloned.1.call-done = bf16[4096,128]{1,0:T(8,128)(2,1)} async-done(((bf16[512,128]{1,0:T(8,128)(2,1)}), bf16[4096,128]{1,0:T(8,128)(2,1)}) %all-gather.4.cloned.1.call-update) | async-done | bytes 1048592 | tf_op jit(solution)/shard_map/all_gather | solution.py:13
  47.2 1.8 multiply_reduce_fusion.1
  49.1 52.3 %all-gather.6.cloned.1.call-done = bf16[8192,128]{1,0:T(8,128)(2,1)} async-done(((bf16[512,128]{1,0:T(8,128)(2,1)}), bf16[8192,128]{1,0:T(8,128)(2,1)}) %all-gather.6.cloned.1.call-update) | async-done | bytes 2097168 | tf_op jit(solution)/shard_map/all_gather | solution.py:21
  101.4 2.9 multiply_reduce_fusion
  104.3 45.9 %all-gather.8.cloned.1.call-done = bf16[8192,128]{1,0:T(8,128)(2,1)} async-done(((bf16[512,128]{1,0:T(8,128)(2,1)}), bf16[8192,128]{1,0:T(8,128)(2,1)}) %all-gather.8.cloned.1.call-update) | async-done | bytes 2097168 | tf_op jit(solution)/shard_map/all_gather | solution.py:22
  150.2 56.3 %while.10 = (s32[]{:T(128)}, f32[8,512,128]{2,1,0:T(8,128)}, f32[8,512]{1,0:T(8,128)S(1)}, f32[8192]{0:T(1024)S(1)}, bf16[8,512,128]{2,1,0:T(8,128)(2,1)}, /*ind...) while((s32[]{:T(128)}, f32[8,512,128]{2,1,0:T(8,128)}, f32[8,512]{1,0:T(8,128)S(1)}, ...), condition=%wide.region_3.4_spmd, body=%wide.region_2.3_spmd.sunk | while | flops 2168455168 | bytes 4627545 | solution.py:34
  150.2 7.0 %fusion.27 = f32[8,512,128]{2,1,0:T(8,128)} fusion(f32[8,512,128]{2,1,0:T(8,128)} %get-tuple-element.106, s32[]{:T(128)} %get-tuple-element.105, bf16[8192,128]{1,0:T(8,128)(2,1)} %get-tuple-element.119, bf16[8192,128]{1,0:T(8,128)(2,1)S(1)} %get-tuple-element.118, f32[8192]{0:T(1024)S(1)} %get-tuple-element.116, f32[512]{0:T(512)S(1)} %bitcast.37, ...), kind=kOutput, calls=%fused_computation.3.clone.1 | convolution fusion | flops 2168455168 | bytes 4623360 | tf_op jit(solution)/shard_map/while/body/eval_jaxpr/dot_general | solution.py:32
  157.2 7.0 %fusion.27 = f32[8,512,128]{2,1,0:T(8,128)} fusion(f32[8,512,128]{2,1,0:T(8,128)} %get-tuple-element.106, s32[]{:T(128)} %get-tuple-element.105, bf16[8192,128]{1,0:T(8,128)(2,1)} %get-tuple-element.119, bf16[8192,128]{1,0:T(8,128)(2,1)S(1)} %get-tuple-element.118, f32[8192]{0:T(1024)S(1)} %get-tuple-element.116, f32[512]{0:T(512)S(1)} %bitcast.37, ...), kind=kOutput, calls=%fused_computation.3.clone.1 | convolution fusion | flops 2168455168 | bytes 4623360 | tf_op jit(solution)/shard_map/while/body/eval_jaxpr/dot_general | solution.py:32
  164.3 7.0 %fusion.27 = f32[8,512,128]{2,1,0:T(8,128)} fusion(f32[8,512,128]{2,1,0:T(8,128)} %get-tuple-element.106, s32[]{:T(128)} %get-tuple-element.105, bf16[8192,128]{1,0:T(8,128)(2,1)} %get-tuple-element.119, bf16[8192,128]{1,0:T(8,128)(2,1)S(1)} %get-tuple-element.118, f32[8192]{0:T(1024)S(1)} %get-tuple-element.116, f32[512]{0:T(512)S(1)} %bitcast.37, ...), kind=kOutput, calls=%fused_computation.3.clone.1 | convolution fusion | flops 2168455168 | bytes 4623360 | tf_op jit(solution)/shard_map/while/body/eval_jaxpr/dot_general | solution.py:32
  171.3 7.0 %fusion.27 = f32[8,512,128]{2,1,0:T(8,128)} fusion(f32[8,512,128]{2,1,0:T(8,128)} %get-tuple-element.106, s32[]{:T(128)} %get-tuple-element.105, bf16[8192,128]{1,0:T(8,128)(2,1)} %get-tuple-element.119, bf16[8192,128]{1,0:T(8,128)(2,1)S(1)} %get-tuple-element.118, f32[8192]{0:T(1024)S(1)} %get-tuple-element.116, f32[512]{0:T(512)S(1)} %bitcast.37, ...), kind=kOutput, calls=%fused_computation.3.clone.1 | convolution fusion | flops 2168455168 | bytes 4623360 | tf_op jit(solution)/shard_map/while/body/eval_jaxpr/dot_general | solution.py:32
  178.3 7.0 %fusion.27 = f32[8,512,128]{2,1,0:T(8,128)} fusion(f32[8,512,128]{2,1,0:T(8,128)} %get-tuple-element.106, s32[]{:T(128)} %get-tuple-element.105, bf16[8192,128]{1,0:T(8,128)(2,1)} %get-tuple-element.119, bf16[8192,128]{1,0:T(8,128)(2,1)S(1)} %get-tuple-element.118, f32[8192]{0:T(1024)S(1)} %get-tuple-element.116, f32[512]{0:T(512)S(1)} %bitcast.37, ...), kind=kOutput, calls=%fused_computation.3.clone.1 | convolution fusion | flops 2168455168 | bytes 4623360 | tf_op jit(solution)/shard_map/while/body/eval_jaxpr/dot_general | solution.py:32
  185.4 7.0 %fusion.27 = f32[8,512,128]{2,1,0:T(8,128)} fusion(f32[8,512,128]{2,1,0:T(8,128)} %get-tuple-element.106, s32[]{:T(128)} %get-tuple-element.105, bf16[8192,128]{1,0:T(8,128)(2,1)} %get-tuple-element.119, bf16[8192,128]{1,0:T(8,128)(2,1)S(1)} %get-tuple-element.118, f32[8192]{0:T(1024)S(1)} %get-tuple-element.116, f32[512]{0:T(512)S(1)} %bitcast.37, ...), kind=kOutput, calls=%fused_computation.3.clone.1 | convolution fusion | flops 2168455168 | bytes 4623360 | tf_op jit(solution)/shard_map/while/body/eval_jaxpr/dot_general | solution.py:32
  192.4 7.0 %fusion.27 = f32[8,512,128]{2,1,0:T(8,128)} fusion(f32[8,512,128]{2,1,0:T(8,128)} %get-tuple-element.106, s32[]{:T(128)} %get-tuple-element.105, bf16[8192,128]{1,0:T(8,128)(2,1)} %get-tuple-element.119, bf16[8192,128]{1,0:T(8,128)(2,1)S(1)} %get-tuple-element.118, f32[8192]{0:T(1024)S(1)} %get-tuple-element.116, f32[512]{0:T(512)S(1)} %bitcast.37, ...), kind=kOutput, calls=%fused_computation.3.clone.1 | convolution fusion | flops 2168455168 | bytes 4623360 | tf_op jit(solution)/shard_map/while/body/eval_jaxpr/dot_general | solution.py:32
  199.4 7.0 %fusion.27 = f32[8,512,128]{2,1,0:T(8,128)} fusion(f32[8,512,128]{2,1,0:T(8,128)} %get-tuple-element.106, s32[]{:T(128)} %get-tuple-element.105, bf16[8192,128]{1,0:T(8,128)(2,1)} %get-tuple-element.119, bf16[8192,128]{1,0:T(8,128)(2,1)S(1)} %get-tuple-element.118, f32[8192]{0:T(1024)S(1)} %get-tuple-element.116, f32[512]{0:T(512)S(1)} %bitcast.37, ...), kind=kOutput, calls=%fused_computation.3.clone.1 | convolution fusion | flops 2168455168 | bytes 4623360 | tf_op jit(solution)/shard_map/while/body/eval_jaxpr/dot_general | solution.py:32
  206.6 77.2 %all-reduce.4.cloned.1.call-done = f32[4096,128]{1,0:T(8,128)} async-done(((f32[4096,128]{1,0:T(8,128)}), f32[4096,128]{1,0:T(8,128)}) %all-reduce.4.cloned.1.call-update) | async-done | bytes 2097168 | tf_op jit(solution)/shard_map/psum | solution.py:36
  283.8 1.0 constant_dynamic-slice_fusion.1
  284.8 1.2 fusion.14
  286.2 130.2 %all-reduce.6.cloned.1.call-done = f32[128,128]{0,1:T(8,128)} async-done(((f32[128,128]{0,1:T(8,128)}), f32[128,128]{0,1:T(8,128)}) %all-reduce.6.cloned.1.call-update) | async-done | bytes 65552 | tf_op jit(solution)/shard_map/psum | solution.py:42
  416.5 72.0 %all-reduce.8.cloned.1.call-done = f32[128,128]{0,1:T(8,128)} async-done(((f32[128,128]{0,1:T(8,128)}), f32[128,128]{0,1:T(8,128)}) %all-reduce.8.cloned.1.call-update) | async-done | bytes 65552 | tf_op jit(solution)/shard_map/psum | solution.py:42
  488.5 0.9 copy.5
  489.4 0.9 fusion.13
  490.3 11.7 %cholesky.16 = f32[128,128]{1,0:T(8,128)S(1)} custom-call(f32[128,128]{1,0:T(8,128)S(1)} %fusion.13), custom_call_target="Cholesky" | custom-call | tf_op jit(solution)/shard_map/jit(cholesky)/cholesky | solution.py:43
  503.3 9.8 %custom-call.7 = f32[1,128,128]{1,2,0:T(8,128)S(1)} custom-call(f32[1,128,128]{2,1,0:T(8,128)S(1)} %fusion.11), custom_call_target="InvertDiagBlocksLowerTriangular" | custom-call | tf_op jit(solution)/shard_map/jit(_solve_triangular)/triangular_solve | solution.py:44
  513.1 1.1 convolution_multiply_fusion
  (29 shorter events, 3.9 us)
Async XLA Ops:
  7.2 40.1 %all-gather.4.cloned.1.call-start = ((), (), s32[]{:S(2)}) async-start(), calls=%async_computation | async-start | bytes 1179648 | tf_op jit(solution)/shard_map/all_gather | solution.py:13
  7.9 93.5 %all-gather.6.cloned.1.call-start = ((), (), s32[]{:S(2)}) async-start(), calls=%async_computation.1 | async-start | bytes 2228224 | tf_op jit(solution)/shard_map/all_gather | solution.py:21
  8.6 141.6 %all-gather.8.cloned.1.call-start = ((), (), s32[]{:S(2)}) async-start(), calls=%async_computation.2 | async-start | bytes 2228224 | tf_op jit(solution)/shard_map/all_gather | solution.py:22
  9.4 274.4 %all-reduce.4.cloned.1.call-start = ((), (), s32[]{:S(2)}) async-start(), calls=%async_computation.3 | async-start | bytes 4194304 | tf_op jit(solution)/shard_map/psum | solution.py:36
  101.4 48.8 %copy-start.1 = (bf16[8192,128]{1,0:T(8,128)(2,1)S(1)}, bf16[8192,128]{1,0:T(8,128)(2,1)}, u32[]{:S(2)}) copy-start(bf16[8192,128]{1,0:T(8,128)(2,1)} %all-gather.6.cloned.1.call-done) | copy-start | bytes 6291460
  206.5 209.9 %all-reduce.6.cloned.1.call-start = ((), (), s32[]{:S(2)}) async-start(), calls=%async_computation.4 | async-start | bytes 131072 | tf_op jit(solution)/shard_map/psum | solution.py:42
  284.8 229.5 %copy-start = (f32[512,128]{1,0:T(8,128)}, f32[512,128]{1,0:T(8,128)S(1)}, u32[]{:S(2)}) copy-start(f32[512,128]{1,0:T(8,128)S(1)} %constant_dynamic-slice_fusion.1) | copy-start | bytes 786436
  286.0 202.5 %all-reduce.8.cloned.1.call-start = ((), (), s32[]{:S(2)}) async-start(), calls=%async_computation.5 | async-start | bytes 131072 | tf_op jit(solution)/shard_map/psum | solution.py:42
Sparse Core Ops, SparseCore 0:
  9.6 37.5 all-gather.3
  49.7 51.6 all-gather.5
  103.9 46.2 all-gather.7
  206.6 77.1 all-reduce.3
  286.7 129.7 all-reduce.5
  418.9 69.5 all-reduce.7
